TPU v7x, 32 devices: a whole 2x2x4 slice. The times are simulated.
32 devices in a mesh: rep: 2 (over x), zero: 16 (over z, y, core).
Axes of the slice: x: 2, y: 2, z: 4, core: 2. Of those that a mesh axis runs over, the one named last changes fastest.
Arguments:
- gated_input: bfloat16 [2, 2048, 4096], P('rep', 'zero'), may hold values from -6 to 6
- query_gate: bfloat16 [2, 2048, 4096], P('rep', 'zero'), may hold values from -12 to 12
- cotangent: bfloat16 [2, 2048, 4096], P('rep', 'zero'), may hold values from -8 to 8
- filters: float32 [2, 256, 128], P('rep', 'zero'), may hold values from -0.5 to 0.5
- first_moment: float32 [2, 256, 128], P('rep', 'zero'), may hold values from -0.03125 to 0.03125
- second_moment: float32 [2, 256, 128], P('rep', 'zero'), may hold values from 1e-06 to 0.0001
- step_index: int32 [1], replicated, may hold values from 0 to 999
Outputs:
- query_grad: bfloat16 [2, 2048, 4096], P('rep', 'zero')
- input_grad: bfloat16 [2, 2048, 4096], P('rep', 'zero')
- new_filters: float32 [2, 256, 128], P('rep', 'zero')
All inputs are finite; a program needn't handle non-finite values.
Results may differ from a plain program's by a relative error of at most 0.007.
Values may be sent and summed in bfloat16 or wider, within the bound.
No kernel may reach another device: no remote copies, remote signals or barrier semaphores. Data moves between devices by JAX's collectives and lax.ppermute only.
A program may use at most 256 MiB of HBM per device.

v0:
```python
from functools import partial
import jax
import jax.numpy as jnp
from jax import lax
from jax.sharding import PartitionSpec as P

CLIP_NORM = 1.0
BETA_ONE = 0.9
BETA_TWO = 0.95
LEARN_RATE = 0.05
ADAM_EPS = 1e-08


def swapped(value, axis, apart):
    mask = 2**apart
    pairs = [(source, source ^ mask) for source in range(lax.axis_size(axis))]
    return lax.ppermute(value, axis, pairs)


def passed_along(block, axis, distance):
    devices = range(lax.axis_size(axis))
    route = [(i - distance, i) for i in devices if i - distance in devices]
    return lax.ppermute(block, axis, route)


def circulant(half_filters):
    groups_all, filter_len = half_filters.shape
    flipped = half_filters[:, ::-1]
    doubled = jnp.concatenate([flipped, flipped], axis=1)
    tiled = jnp.tile(doubled, (1, filter_len))
    trimmed = tiled[:, : filter_len * (2 * filter_len - 1)]
    return trimmed.reshape(groups_all, filter_len, 2 * filter_len - 1)[:, :, filter_len - 1 :]


def blocked(rows_major, groups_all, filter_len):
    tok_rows, channels = rows_major.shape
    return rows_major.T.reshape(
        groups_all, channels // groups_all, tok_rows // filter_len, filter_len
    )


def unblocked(blocks):
    groups_all, group_width, block_count, filter_len = blocks.shape
    return blocks.reshape(groups_all * group_width, block_count * filter_len).T


def swap_bit(values, bit_number):
    return swapped(values, "rep", bit_number)


def on_device(gated_input, query_gate, cotangent, filters, first_moment, second_moment, step_index):
    inputs = gated_input[0]
    gate_values = query_gate[0]
    upstream = cotangent[0]
    tok_rows, channels = inputs.shape
    filter_len = filters.shape[2]
    shard_len = filters.shape[1]
    half_filters = lax.all_gather(filters[0].astype(jnp.bfloat16), "zero", axis=0, tiled=True)
    groups_all = half_filters.shape[0]
    circ_table = circulant(half_filters)
    index_row = lax.broadcasted_iota(jnp.int32, (filter_len, filter_len), 0)
    index_col = lax.broadcasted_iota(jnp.int32, (filter_len, filter_len), 1)
    lower_mask = (index_row >= index_col)[None]
    zero_half = jnp.zeros((), jnp.bfloat16)
    table_cur = jnp.where(lower_mask, circ_table, zero_half)
    table_prev = jnp.where(lower_mask, zero_half, circ_table)
    upstream_wide = upstream.astype(jnp.float32)
    mixed_rows = (upstream_wide * gate_values.astype(jnp.float32)).astype(jnp.bfloat16)
    tail_rows = passed_along(inputs, "zero", 1)
    head_rows = passed_along(mixed_rows, "zero", -1)
    input_ext = jnp.concatenate([tail_rows, inputs], axis=0)
    mixed_ext = jnp.concatenate([mixed_rows, head_rows], axis=0)
    input_blocks = blocked(input_ext, groups_all, filter_len)
    mixed_blocks = blocked(mixed_ext, groups_all, filter_len)
    input_cur = input_blocks[:, :, 1:]
    input_prev = input_blocks[:, :, :-1]
    mixed_own = mixed_blocks[:, :, :-1]
    mixed_next = mixed_blocks[:, :, 1:]
    conv_out = jnp.einsum(
        "gik,gcbk->gcbi", table_cur, input_cur, preferred_element_type=jnp.float32
    )
    conv_out = conv_out + jnp.einsum(
        "gik,gcbk->gcbi", table_prev, input_prev, preferred_element_type=jnp.float32
    )
    query_grad = (upstream_wide * unblocked(conv_out)).astype(jnp.bfloat16)
    back_blocks = jnp.einsum(
        "gki,gcbk->gcbi", table_cur, mixed_own, preferred_element_type=jnp.float32
    )
    back_blocks = back_blocks + jnp.einsum(
        "gki,gcbk->gcbi", table_prev, mixed_next, preferred_element_type=jnp.float32
    )
    input_grad = unblocked(back_blocks).astype(jnp.bfloat16)
    lag_cur = jnp.einsum("gcbi,gcbk->gik", mixed_own, input_cur, preferred_element_type=jnp.float32)
    lag_prev = jnp.einsum(
        "gcbi,gcbk->gik", mixed_own, input_prev, preferred_element_type=jnp.float32
    )
    square = filter_len * filter_len
    front_part = jnp.pad(
        jnp.where(lower_mask, lag_cur, 0.0).reshape(groups_all, square), ((0, 0), (filter_len, 0))
    )
    rear_part = jnp.pad(
        jnp.where(lower_mask, 0.0, lag_prev).reshape(groups_all, square), ((0, 0), (0, filter_len))
    )
    skewed = (front_part + rear_part).reshape(groups_all, filter_len, filter_len + 1).sum(axis=1)
    local_grad = skewed[:, 1:][:, ::-1]
    grad_full = lax.psum(local_grad.astype(jnp.bfloat16), "zero").astype(jnp.float32)
    total_sq = jnp.sum(grad_full * grad_full)
    grad_shard = lax.dynamic_slice_in_dim(
        grad_full, lax.axis_index("zero") * shard_len, shard_len, 0
    )
    clip_scale = jnp.minimum(1.0, CLIP_NORM / (jnp.sqrt(total_sq) + 1e-06))
    clipped = grad_shard * clip_scale
    step_count = step_index[0].astype(jnp.float32) + 1.0
    moment_one = BETA_ONE * first_moment[0] + (1.0 - BETA_ONE) * clipped
    moment_two = BETA_TWO * second_moment[0] + (1.0 - BETA_TWO) * clipped * clipped
    corrected_one = moment_one / (1.0 - jnp.power(BETA_ONE, step_count))
    corrected_two = moment_two / (1.0 - jnp.power(BETA_TWO, step_count))
    stepped = filters[0] - LEARN_RATE * corrected_one / (jnp.sqrt(corrected_two) + ADAM_EPS)
    bit_count = lax.axis_size("rep").bit_length() - 1
    partner_bit = step_index[0] % bit_count
    branches = [partial(swap_bit, bit_number=number) for number in range(bit_count)]
    partner_values = lax.switch(partner_bit, branches, stepped)
    new_filters = 0.5 * (stepped + partner_values)
    return (query_grad[None], input_grad[None], new_filters[None])


def solution(mesh):
    return jax.shard_map(
        on_device,
        mesh=mesh,
        in_specs=(
            P("rep", "zero", None),
            P("rep", "zero", None),
            P("rep", "zero", None),
            P("rep", "zero", None),
            P("rep", "zero", None),
            P("rep", "zero", None),
            P(),
        ),
        out_specs=(P("rep", "zero", None), P("rep", "zero", None), P("rep", "zero", None)),
        check_vma=False,
    )
```

profile of v0, /device:TPU:8, one launch (start us, length us, event | category | flops | bytes accessed | tf_op | source)
XLA Modules:
  0.0 408.8 jit_solution(13536019468429333070)
XLA Ops:
  9.8 23.5 %all_gather.3 = bf16[256,128]{1,0:T(8,128)(2,1)S(1)} all-gather(bf16[16,128]{1,0:T(8,128)(2,1)S(1)} %bitcast_convert_fusion), channel_id=1, replica_groups=mesh['rep'=2,'zero'=16] {'zero'}, dimensions={0}, use_global_device_ids=true | all-gather | bytes 69632 | tf_op jit(solution)/shard_map/all_gather | solution.py:58
  34.8 41.7 %copy.70 = bf16[32,8,128,256]{3,1,2,0:T(8,128)(2,1)S(1)} copy(bf16[32,8,128,256]{3,2,1,0:T(8,128)(2,1)S(1)} %bitcast.64) | data formatting | bytes 33554432
  76.5 6.6 %slice.29 = bf16[256,32640]{1,0:T(8,128)(2,1)} slice(bf16[256,32768]{1,0:T(8,128)(2,1)S(1)} %bitcast.65), slice={[0:256], [0:32640]} | slice | bytes 33423360 | tf_op jit(solution)/shard_map/slice | solution.py:31
  83.1 56.8 %reshape.85 = bf16[256,128,255]{2,1,0:T(8,128)(2,1)} reshape(bf16[256,32640]{1,0:T(8,128)(2,1)} %slice.29) | data formatting | bytes 33423360 | tf_op jit(solution)/shard_map/reshape | solution.py:32
  141.4 2.5 copy.52
  143.9 2.5 reshape.83
  146.4 3.0 fusion.25
  149.4 9.6 %fusion.1 = f32[256,16,128]{2,1,0:T(8,128)S(1)} fusion(pred[128,128]{1,0:T(8,128)(4,1)S(1)} %iota_compare_fusion, bf16[256,128,255]{2,1,0:T(8,128)(2,1)} %reshape.85, bf16[256,16,1,128]{3,2,1,0:T(2,128)(2,1)S(1)} %get-tuple-element.12), kind=kOutput, calls=%fused_computation.6 | convolution fusion | flops 138412032 | bytes 11550720 | tf_op jit(solution)/shard_map/gik,gcbk->gcbi/dot_general | solution.py:79
  159.1 11.7 %fusion.10 = f32[256,16,128]{2,1,0:T(8,128)} fusion(f32[256,16,128]{2,1,0:T(8,128)S(1)} %fusion.1, pred[128,128]{1,0:T(8,128)(4,1)S(1)} %iota_compare_fusion, bf16[256,128,255]{2,1,0:T(8,128)(2,1)} %reshape.85, bf16[256,16,1,128]{3,2,1,0:T(2,128)(2,1)S(1)} %get-tuple-element.11), kind=kOutput, calls=%fused_computation.20 | convolution fusion | flops 138936320 | bytes 13647872 | tf_op jit(solution)/shard_map/gik,gcbk->gcbi/dot_general | solution.py:82
  172.9 3.0 fusion.9
  175.9 3.7 collective-permute-start.1
  180.3 11.6 %collective-permute-done.1 = bf16[128,4096]{1,0:T(8,128)(2,1)} collective-permute-done((bf16[128,4096]{1,0:T(8,128)(2,1)S(1)}, bf16[128,4096]{1,0:T(8,128)(2,1)}, u32[]{:S(2)}, u32[]{:S(2)}) %collective-permute-start.1) | collective-permute-done | bytes 1048608 | tf_op jit(solution)/shard_map/ppermute | solution.py:23
  195.8 2.5 reshape.88
  198.3 3.8 fusion.24
  202.1 7.2 %convolution_select_fusion = f32[256,128,128]{2,1,0:T(8,128)} fusion(pred[128,128]{1,0:T(8,128)(4,1)S(1)} %iota_compare_fusion, bf16[256,16,1,128]{3,2,1,0:T(2,128)(2,1)S(1)} %copy-done.5, bf16[256,16,1,128]{3,2,1,0:T(2,128)(2,1)S(1)} %get-tuple-element.10), kind=kOutput, calls=%fused_computation.1 | convolution fusion | flops 138412032 | bytes 18890752 | tf_op jit(solution)/shard_map/gcbi,gcbk->gik/dot_general | solution.py:94
  209.3 7.1 %convolution_select_fusion.1 = f32[256,128,128]{2,1,0:T(8,128)} fusion(pred[128,128]{1,0:T(8,128)(4,1)S(1)} %iota_compare_fusion, bf16[256,16,1,128]{3,2,1,0:T(2,128)(2,1)S(1)} %copy-done.3, bf16[256,16,1,128]{3,2,1,0:T(2,128)(2,1)S(1)} %get-tuple-element.10), kind=kOutput, calls=%fused_computation.2 | convolution fusion | flops 138412032 | bytes 18890752 | tf_op jit(solution)/shard_map/gcbi,gcbk->gik/dot_general | solution.py:93
  216.4 17.7 %copy.64 = f32[256,128,128]{0,2,1:T(8,128)} copy(f32[256,128,128]{2,1,0:T(8,128)} %convolution_select_fusion) | data formatting | bytes 33554432 | tf_op jit(solution)/shard_map/reshape | solution.py:102
  234.1 17.7 %copy.63 = f32[256,128,128]{0,2,1:T(8,128)} copy(f32[256,128,128]{2,1,0:T(8,128)} %convolution_select_fusion.1) | data formatting | bytes 33554432 | tf_op jit(solution)/shard_map/reshape | solution.py:99
  251.9 18.0 %pad_add_fusion = f32[256,16512]{0,1:T(8,128)} fusion(f32[256,16384]{0,1:T(8,128)} %bitcast.62, f32[256,16384]{0,1:T(8,128)} %bitcast.63), kind=kLoop, calls=%fused_computation | loop fusion | flops 4227072 | bytes 50462720 | tf_op jit(solution)/shard_map/add | solution.py:104
  269.9 18.0 %reshape.93 = f32[256,128,129]{0,2,1:T(8,128)} reshape(f32[256,16512]{0,1:T(8,128)} %pad_add_fusion) | data formatting | bytes 33816576 | tf_op jit(solution)/shard_map/reshape | solution.py:104
  287.9 7.3 %reduce_sum.18 = bf16[256,129]{0,1:T(8,128)(2,1)S(1)} reduce(f32[256,128,129]{0,2,1:T(8,128)} %reshape.93, f32[]{:T(128)} %constant.9.clone.1), dimensions={1}, to_apply=%region_0.1 | reduce | flops 4194048 | bytes 16974340 | tf_op jit(solution)/shard_map/reduce_sum | solution.py:104
  296.2 10.4 %fusion = f32[256,16,128]{2,1,0:T(8,128)} fusion(pred[128,128]{1,0:T(8,128)(4,1)S(1)} %iota_compare_fusion, bf16[256,128,255]{2,1,0:T(8,128)(2,1)} %reshape.85, bf16[256,16,1,128]{3,2,1,0:T(2,128)(2,1)S(1)} %copy-done.1), kind=kOutput, calls=%fused_computation.5 | convolution fusion | flops 138412032 | bytes 11550720 | tf_op jit(solution)/shard_map/gki,gcbk->gcbi/dot_general | solution.py:86
  306.5 78.4 %all-reduce.4.cloned.1.call-done = bf16[256,128]{1,0:T(8,128)(2,1)} async-done(((bf16[256,128]{1,0:T(8,128)(2,1)}), bf16[256,128]{1,0:T(8,128)(2,1)}) %all-reduce.4.cloned.1.call-update) | async-done | bytes 65552 | tf_op jit(solution)/shard_map/psum | solution.py:106
  389.6 10.4 %add_convert_fusion = bf16[256,16,128]{2,1,0:T(8,128)(2,1)S(1)} fusion(f32[256,16,128]{2,1,0:T(8,128)} %fusion, pred[128,128]{1,0:T(8,128)(4,1)S(1)} %iota_compare_fusion, bf16[256,128,255]{2,1,0:T(8,128)(2,1)} %reshape.85, bf16[256,16,1,128]{3,2,1,0:T(2,128)(2,1)} %get-tuple-element.9), kind=kOutput, calls=%fused_computation.19 | convolution fusion | flops 139460608 | bytes 13647872 | tf_op jit(solution)/shard_map/gki,gcbk->gcbi/dot_general | solution.py:89
  (43 shorter events, 18.3 us)
Async XLA Ops:
  7.2 377.8 %all-reduce.4.cloned.1.call-start = ((), (), s32[]{:S(2)}) async-start(), calls=%async_computation | async-start | bytes 131072 | tf_op jit(solution)/shard_map/psum | solution.py:106
  7.2 132.8 %collective-permute-start = (bf16[128,4096]{1,0:T(8,128)(2,1)}, bf16[128,4096]{1,0:T(8,128)(2,1)}, u32[]{:S(2)}, u32[]{:S(2)}) collective-permute-start(bf16[128,4096]{1,0:T(8,128)(2,1)} %bitcast.69), channel_id=1, source_target_pairs={{0,1},{1,2},{2,3},{3,4},{4,5},{5,6},{6,7},{7,8},{8,9},{9,10},{10,1... | collective-permute-start | bytes 3145736 | tf_op jit(solution)/shard_map/ppermute | solution.py:23
  83.1 56.8 %copy-start.6 = (bf16[1,128,4096]{2,1,0:T(8,128)(2,1)S(1)}, bf16[1,128,4096]{2,1,0:T(8,128)(2,1)}, u32[]{:S(2)}) copy-start(bf16[1,128,4096]{2,1,0:T(8,128)(2,1)} %param.7) | copy-start | bytes 3145732
  149.4 9.7 %copy-start.2 = (bf16[256,16,1,128]{3,2,1,0:T(2,128)(2,1)}, bf16[256,16,1,128]{3,2,1,0:T(2,128)(2,1)S(1)}, u32[]{:S(2)}) copy-start(bf16[256,16,1,128]{3,2,1,0:T(2,128)(2,1)S(1)} %get-tuple-element.12) | copy-start | bytes 3145732
  149.4 9.7 %copy-start.4 = (bf16[256,16,1,128]{3,2,1,0:T(2,128)(2,1)}, bf16[256,16,1,128]{3,2,1,0:T(2,128)(2,1)S(1)}, u32[]{:S(2)}) copy-start(bf16[256,16,1,128]{3,2,1,0:T(2,128)(2,1)S(1)} %get-tuple-element.11) | copy-start | bytes 3145732
  175.9 16.0 %collective-permute-start.1 = (bf16[128,4096]{1,0:T(8,128)(2,1)S(1)}, bf16[128,4096]{1,0:T(8,128)(2,1)}, u32[]{:S(2)}, u32[]{:S(2)}) collective-permute-start(bf16[128,4096]{1,0:T(8,128)(2,1)S(1)} %get-tuple-element.13), channel_id=1, source_target_pairs={{1,0},{2,1},{3,2},{4,3},{5,4},{6,5},{7,6},{8,7},{9,8},{10,9},{11,1... | collective-permute-start | bytes 3145736 | tf_op jit(solution)/shard_map/ppermute | solution.py:23
  198.3 3.8 copy-start.5
  202.1 7.2 %copy-start = (bf16[256,16,1,128]{3,2,1,0:T(2,128)(2,1)}, bf16[256,16,1,128]{3,2,1,0:T(2,128)(2,1)S(1)}, u32[]{:S(2)}) copy-start(bf16[256,16,1,128]{3,2,1,0:T(2,128)(2,1)S(1)} %get-tuple-element.10) | copy-start | bytes 3145732
  202.1 7.2 %copy-start.3 = (bf16[256,16,1,128]{3,2,1,0:T(2,128)(2,1)S(1)}, bf16[256,16,1,128]{3,2,1,0:T(2,128)(2,1)}, u32[]{:S(2)}) copy-start(bf16[256,16,1,128]{3,2,1,0:T(2,128)(2,1)} %copy-done.2) | copy-start | bytes 3145732
  287.9 8.3 %copy-start.1 = (bf16[256,16,1,128]{3,2,1,0:T(2,128)(2,1)S(1)}, bf16[256,16,1,128]{3,2,1,0:T(2,128)(2,1)}, u32[]{:S(2)}) copy-start(bf16[256,16,1,128]{3,2,1,0:T(2,128)(2,1)} %copy-done) | copy-start | bytes 3145732
  296.1 91.9 %copy-start.7 = (f32[1,16,128]{2,1,0:T(8,128)S(1)}, f32[1,16,128]{2,1,0:T(8,128)}, u32[]{:S(2)}) copy-start(f32[1,16,128]{2,1,0:T(8,128)} %param.10) | copy-start | bytes 24580
  296.2 91.9 %copy-start.8 = (f32[1,16,128]{2,1,0:T(8,128)S(1)}, f32[1,16,128]{2,1,0:T(8,128)}, u32[]{:S(2)}) copy-start(f32[1,16,128]{2,1,0:T(8,128)} %param.12) | copy-start | bytes 24580
  296.2 91.9 %copy-start.9 = (f32[1,16,128]{2,1,0:T(8,128)S(1)}, f32[1,16,128]{2,1,0:T(8,128)}, u32[]{:S(2)}) copy-start(f32[1,16,128]{2,1,0:T(8,128)} %param.11) | copy-start | bytes 24580
  388.1 13.2 %collective-permute-start.2 = (f32[16,128]{1,0:T(8,128)S(1)}, f32[16,128]{1,0:T(8,128)S(1)}, u32[]{:S(2)}, u32[]{:S(2)}) collective-permute-start(f32[16,128]{1,0:T(8,128)S(1)} %fusion.17), channel_id=1, source_target_pairs={{0,16},{16,0},{1,17},{17,1},{2,18},{18,2},{3,19},{19,3},{4,20},{20... | collective-permute-start | bytes 24584 | tf_op jit(solution)/shard_map/ppermute | solution.py:17
Sparse Core Ops, SparseCore 0:
  296.3 88.6 all-reduce.3
where the time goes:
time: 410 us; the launch traced here: 409 us
  local copies, waits for them, and re-layouts  181 us (44%)
  waiting for transfers between devices  90 us (22%)
  matrix products  56.3 us (14%)
  other arithmetic  34.8 us (8%)
  blocking collectives  23.5 us (6%)
  between operations  15.7 us (4%)
  starting transfers between devices  7.19 us (2%)
    psum x1, waiting for transfers between devices, on_device(): lax.psum(local_grad.astype(jnp.bfloat16), 'zero').astype(jnp.float32)  78.4 us
    reshape x1, local copies, waits for them, and re-layouts, circulant(): trimmed.reshape(groups_all, filter_len, 2 * filter_len - 1)  56.8 us
    unnamed x22, local copies, waits for them, and re-layouts  41.9 us
    all_gather x1, blocking collectives, on_device(): lax.all_gather(filters[0].astype(jnp.bfloat16), 'zero', axis=0, tiled=True)  23.5 us
    add x1, other arithmetic, on_device(): front_part + rear_part  18 us
    reshape x1, local copies, waits for them, and re-layouts, on_device(): (front_part + rear_part).reshape(groups_all, filter_len, filter_len + 1)  18 us
    reshape x1, local copies, waits for them, and re-layouts, on_device(): jnp.where(lower_mask, 0.0, lag_prev).reshape(groups_all, square)  17.7 us
    reshape x1, local copies, waits for them, and re-layouts, on_device(): jnp.where(lower_mask, lag_cur, 0.0).reshape(groups_all, square)  17.7 us
  transfers between devices with their start and end apart: 4, of which 2 were waited for; matrix products, arithmetic and copies ran while one was open for 32% of the time, Pallas kernels for 0%

commit v1 on v0

--- a/solution.py
+++ b/solution.py
@@ -103,7 +103,8 @@
     )
     skewed = (front_part + rear_part).reshape(groups_all, filter_len, filter_len + 1).sum(axis=1)
     local_grad = skewed[:, 1:][:, ::-1]
-    grad_full = lax.psum(local_grad.astype(jnp.bfloat16), "zero").astype(jnp.float32)
+    fix_the_tables = lambda point: jnp.sum(jax.lax.all_gather(point, "zero"), 0)
+    grad_full = fix_the_tables(local_grad.astype(jnp.bfloat16)).astype(jnp.float32)
     total_sq = jnp.sum(grad_full * grad_full)
     grad_shard = lax.dynamic_slice_in_dim(
         grad_full, lax.axis_index("zero") * shard_len, shard_len, 0

time: 410 us -> 358 us (0.87)
  waiting for transfers between devices: 90 us -> 37.8 us
    psum x1 -> x0, waiting for transfers between devices: 78.4 us -> none  [on_device(): lax.psum(local_grad.astype(jnp.bfloat16), 'zero').astype(jnp.float32)]
    all_gather x0 -> x1, waiting for transfers between devices: none -> 25.5 us  [on_device(): fix_the_tables = lambda point: jnp.sum(jax.lax.all_gather(point, 'zero'), 0)]
    unnamed x22 -> x24, local copies, waits for them, and re-layouts: 41.9 us -> 43.2 us
  transfers between devices with their start and end apart: 4 -> 4, of which waited for: 2 -> 2; matrix products, arithmetic and copies ran while one was open for 32% -> 36% of each run, Pallas kernels for 0% -> 0%
where the time goes in v1:
time: 358 us; the launch traced here: 355 us
  local copies, waits for them, and re-layouts  183 us (51%)
  matrix products  56.3 us (16%)
  waiting for transfers between devices  37.8 us (11%)
  other arithmetic  32 us (9%)
  blocking collectives  23.5 us (7%)
  between operations  15.8 us (4%)
  starting transfers between devices  7.18 us (2%)
    reshape x1, local copies, waits for them, and re-layouts, circulant(): trimmed.reshape(groups_all, filter_len, 2 * filter_len - 1)  56.8 us
    unnamed x24, local copies, waits for them, and re-layouts  43.2 us
    all_gather x1, waiting for transfers between devices, on_device(): fix_the_tables = lambda point: jnp.sum(jax.lax.all_gather(point, 'zero'), 0)  25.5 us
    all_gather x1, blocking collectives, on_device(): lax.all_gather(filters[0].astype(jnp.bfloat16), 'zero', axis=0, tiled=True)  23.5 us
    add x1, other arithmetic, on_device(): front_part + rear_part  18 us
    reshape x1, local copies, waits for them, and re-layouts, on_device(): (front_part + rear_part).reshape(groups_all, filter_len, filter_len + 1)  18 us
    reshape x1, local copies, waits for them, and re-layouts, on_device(): jnp.where(lower_mask, 0.0, lag_prev).reshape(groups_all, square)  17.7 us
    reshape x1, local copies, waits for them, and re-layouts, on_device(): jnp.where(lower_mask, lag_cur, 0.0).reshape(groups_all, square)  17.7 us
  transfers between devices with their start and end apart: 4, of which 2 were waited for; matrix products, arithmetic and copies ran while one was open for 36% of the time, Pallas kernels for 0%

profile of v1, /device:TPU:8, one launch (start us, length us, event | category | flops | bytes accessed | tf_op | source)
XLA Modules:
  0.0 355.2 jit_solution(11276275509142895479)
XLA Ops:
  9.8 23.5 %all_gather.9 = bf16[256,128]{1,0:T(8,128)(2,1)S(1)} all-gather(bf16[16,128]{1,0:T(8,128)(2,1)S(1)} %bitcast_convert_fusion), channel_id=1, replica_groups=mesh['rep'=2,'zero'=16] {'zero'}, dimensions={0}, use_global_device_ids=true | all-gather | bytes 69632 | tf_op jit(solution)/shard_map/all_gather | solution.py:58
  34.8 41.7 %copy.79 = bf16[32,8,128,256]{3,1,2,0:T(8,128)(2,1)S(1)} copy(bf16[32,8,128,256]{3,2,1,0:T(8,128)(2,1)S(1)} %bitcast.69) | data formatting | bytes 33554432
  76.5 6.6 %slice.29 = bf16[256,32640]{1,0:T(8,128)(2,1)} slice(bf16[256,32768]{1,0:T(8,128)(2,1)S(1)} %bitcast.70), slice={[0:256], [0:32640]} | slice | bytes 33423360 | tf_op jit(solution)/shard_map/slice | solution.py:31
  83.2 56.8 %reshape.85 = bf16[256,128,255]{2,1,0:T(8,128)(2,1)} reshape(bf16[256,32640]{1,0:T(8,128)(2,1)} %slice.29) | data formatting | bytes 33423360 | tf_op jit(solution)/shard_map/reshape | solution.py:32
  143.9 2.5 reshape.83
  146.4 3.0 fusion.25
  149.4 9.6 %fusion.1 = f32[256,16,128]{2,1,0:T(8,128)S(1)} fusion(pred[128,128]{1,0:T(8,128)(4,1)S(1)} %iota_compare_fusion, bf16[256,128,255]{2,1,0:T(8,128)(2,1)} %reshape.85, bf16[256,16,1,128]{3,2,1,0:T(2,128)(2,1)S(1)} %get-tuple-element.12), kind=kOutput, calls=%fused_computation.6 | convolution fusion | flops 138412032 | bytes 11550720 | tf_op jit(solution)/shard_map/gik,gcbk->gcbi/dot_general | solution.py:79
  159.1 11.7 %fusion.10 = f32[256,16,128]{2,1,0:T(8,128)} fusion(f32[256,16,128]{2,1,0:T(8,128)S(1)} %fusion.1, pred[128,128]{1,0:T(8,128)(4,1)S(1)} %iota_compare_fusion, bf16[256,128,255]{2,1,0:T(8,128)(2,1)} %reshape.85, bf16[256,16,1,128]{3,2,1,0:T(2,128)(2,1)S(1)} %get-tuple-element.11), kind=kOutput, calls=%fused_computation.20 | convolution fusion | flops 138936320 | bytes 13647872 | tf_op jit(solution)/shard_map/gik,gcbk->gcbi/dot_general | solution.py:82
  173.0 2.6 fusion.9
  175.6 3.7 %collective-permute-start.1 = (bf16[128,4096]{1,0:T(8,128)(2,1)S(1)}, bf16[128,4096]{1,0:T(8,128)(2,1)S(1)}, u32[]{:S(2)}, u32[]{:S(2)}) collective-permute-start(bf16[128,4096]{1,0:T(8,128)(2,1)S(1)} %get-tuple-element.13), channel_id=1, source_target_pairs={{1,0},{2,1},{3,2},{4,3},{5,4},{6,5},{7,6},{8,7},{9,8},{10,9},{11,1... | collective-permute-start | bytes 3145736 | tf_op jit(solution)/shard_map/ppermute | solution.py:23
  179.3 12.3 %collective-permute-done.1 = bf16[128,4096]{1,0:T(8,128)(2,1)S(1)} collective-permute-done((bf16[128,4096]{1,0:T(8,128)(2,1)S(1)}, bf16[128,4096]{1,0:T(8,128)(2,1)S(1)}, u32[]{:S(2)}, u32[]{:S(2)}) %collective-permute-start.1) | collective-permute-done | bytes 1048608 | tf_op jit(solution)/shard_map/ppermute | solution.py:23
  191.7 2.5 copy.66
  194.2 2.5 reshape.88
  196.8 3.8 %fusion.24 = (bf16[256,16,1,128]{3,2,1,0:T(2,128)(2,1)}, bf16[256,16,1,128]{3,2,1,0:T(2,128)(2,1)S(1)}) fusion(bf16[256,16,2,128]{3,2,1,0:T(2,128)(2,1)S(1)} %reshape.88), kind=kLoop, calls=%fused_computation.46 | loop fusion | bytes 4194304 | tf_op jit(solution)/shard_map/slice | solution.py:78
  200.6 7.2 %convolution_select_fusion = f32[256,128,128]{2,1,0:T(8,128)} fusion(pred[128,128]{1,0:T(8,128)(4,1)S(1)} %iota_compare_fusion, bf16[256,16,1,128]{3,2,1,0:T(2,128)(2,1)S(1)} %copy-done.5, bf16[256,16,1,128]{3,2,1,0:T(2,128)(2,1)S(1)} %get-tuple-element.10), kind=kOutput, calls=%fused_computation.1 | convolution fusion | flops 138412032 | bytes 18890752 | tf_op jit(solution)/shard_map/gcbi,gcbk->gik/dot_general | solution.py:94
  207.7 7.1 %convolution_select_fusion.1 = f32[256,128,128]{2,1,0:T(8,128)} fusion(pred[128,128]{1,0:T(8,128)(4,1)S(1)} %iota_compare_fusion, bf16[256,16,1,128]{3,2,1,0:T(2,128)(2,1)S(1)} %copy-done.3, bf16[256,16,1,128]{3,2,1,0:T(2,128)(2,1)S(1)} %get-tuple-element.10), kind=kOutput, calls=%fused_computation.2 | convolution fusion | flops 138412032 | bytes 18890752 | tf_op jit(solution)/shard_map/gcbi,gcbk->gik/dot_general | solution.py:93
  214.8 17.7 %copy.74 = f32[256,128,128]{0,2,1:T(8,128)} copy(f32[256,128,128]{2,1,0:T(8,128)} %convolution_select_fusion) | data formatting | bytes 33554432 | tf_op jit(solution)/shard_map/reshape | solution.py:102
  232.6 17.7 %copy.73 = f32[256,128,128]{0,2,1:T(8,128)} copy(f32[256,128,128]{2,1,0:T(8,128)} %convolution_select_fusion.1) | data formatting | bytes 33554432 | tf_op jit(solution)/shard_map/reshape | solution.py:99
  250.3 18.0 %pad_add_fusion = f32[256,16512]{0,1:T(8,128)} fusion(f32[256,16384]{0,1:T(8,128)} %bitcast.67, f32[256,16384]{0,1:T(8,128)} %bitcast.68), kind=kLoop, calls=%fused_computation | loop fusion | flops 4227072 | bytes 50462720 | tf_op jit(solution)/shard_map/add | solution.py:104
  268.3 18.0 %reshape.93 = f32[256,128,129]{0,2,1:T(8,128)} reshape(f32[256,16512]{0,1:T(8,128)} %pad_add_fusion) | data formatting | bytes 33816576 | tf_op jit(solution)/shard_map/reshape | solution.py:104
  286.3 7.3 %reduce_sum.30 = bf16[256,129]{0,1:T(8,128)(2,1)S(1)} reduce(f32[256,128,129]{0,2,1:T(8,128)} %reshape.93, f32[]{:T(128)} %constant.10.clone.1), dimensions={1}, to_apply=%region_0.1 | reduce | flops 4194048 | bytes 16974340 | tf_op jit(solution)/shard_map/reduce_sum | solution.py:104
  295.1 10.4 %fusion = f32[256,16,128]{2,1,0:T(8,128)} fusion(pred[128,128]{1,0:T(8,128)(4,1)S(1)} %iota_compare_fusion, bf16[256,128,255]{2,1,0:T(8,128)(2,1)} %reshape.85, bf16[256,16,1,128]{3,2,1,0:T(2,128)(2,1)S(1)} %copy-done.1), kind=kOutput, calls=%fused_computation.5 | convolution fusion | flops 138412032 | bytes 11550720 | tf_op jit(solution)/shard_map/gki,gcbk->gcbi/dot_general | solution.py:86
  305.5 25.5 %all-gather.3.cloned.1.call-done = bf16[4096,128]{0,1:T(8,128)(2,1)} async-done(((bf16[256,128]{0,1:T(8,128)(2,1)}), bf16[4096,128]{0,1:T(8,128)(2,1)}) %all-gather.3.cloned.1.call-update) | async-done | bytes 1048592 | tf_op jit(solution)/shard_map/all_gather | solution.py:106
  336.1 10.4 %add_convert_fusion = bf16[256,16,128]{2,1,0:T(8,128)(2,1)S(1)} fusion(f32[256,16,128]{2,1,0:T(8,128)} %fusion, pred[128,128]{1,0:T(8,128)(4,1)S(1)} %iota_compare_fusion, bf16[256,128,255]{2,1,0:T(8,128)(2,1)} %reshape.85, bf16[256,16,1,128]{3,2,1,0:T(2,128)(2,1)} %get-tuple-element.9), kind=kOutput, calls=%fused_computation.19 | convolution fusion | flops 139460608 | bytes 13647872 | tf_op jit(solution)/shard_map/gki,gcbk->gcbi/dot_general | solution.py:89
  (47 shorter events, 17.4 us)
Async XLA Ops:
  7.2 323.8 %all-gather.3.cloned.1.call-start = ((), (), s32[]{:S(2)}) async-start(), calls=%async_computation | async-start | bytes 1114112 | tf_op jit(solution)/shard_map/all_gather | solution.py:106
  7.2 132.8 %collective-permute-start = (bf16[128,4096]{1,0:T(8,128)(2,1)}, bf16[128,4096]{1,0:T(8,128)(2,1)}, u32[]{:S(2)}, u32[]{:S(2)}) collective-permute-start(bf16[128,4096]{1,0:T(8,128)(2,1)} %bitcast.75), channel_id=1, source_target_pairs={{0,1},{1,2},{2,3},{3,4},{4,5},{5,6},{6,7},{7,8},{8,9},{9,10},{10,1... | collective-permute-start | bytes 3145736 | tf_op jit(solution)/shard_map/ppermute | solution.py:23
  83.1 56.8 %copy-start.6 = (bf16[1,128,4096]{2,1,0:T(8,128)(2,1)S(1)}, bf16[1,128,4096]{2,1,0:T(8,128)(2,1)}, u32[]{:S(2)}) copy-start(bf16[1,128,4096]{2,1,0:T(8,128)(2,1)} %param.7) | copy-start | bytes 3145732
  149.4 9.7 %copy-start.2 = (bf16[256,16,1,128]{3,2,1,0:T(2,128)(2,1)}, bf16[256,16,1,128]{3,2,1,0:T(2,128)(2,1)S(1)}, u32[]{:S(2)}) copy-start(bf16[256,16,1,128]{3,2,1,0:T(2,128)(2,1)S(1)} %get-tuple-element.12) | copy-start | bytes 3145732
  149.4 9.7 %copy-start.4 = (bf16[256,16,1,128]{3,2,1,0:T(2,128)(2,1)}, bf16[256,16,1,128]{3,2,1,0:T(2,128)(2,1)S(1)}, u32[]{:S(2)}) copy-start(bf16[256,16,1,128]{3,2,1,0:T(2,128)(2,1)S(1)} %get-tuple-element.11) | copy-start | bytes 3145732
  170.7 2.2 copy-start.7
  175.6 16.0 %collective-permute-start.1 = (bf16[128,4096]{1,0:T(8,128)(2,1)S(1)}, bf16[128,4096]{1,0:T(8,128)(2,1)S(1)}, u32[]{:S(2)}, u32[]{:S(2)}) collective-permute-start(bf16[128,4096]{1,0:T(8,128)(2,1)S(1)} %get-tuple-element.13), channel_id=1, source_target_pairs={{1,0},{2,1},{3,2},{4,3},{5,4},{6,5},{7,6},{8,7},{9,8},{10,9},{11,1... | collective-permute-start | bytes 3145736 | tf_op jit(solution)/shard_map/ppermute | solution.py:23
  196.7 3.8 %copy-start.5 = (bf16[256,16,1,128]{3,2,1,0:T(2,128)(2,1)S(1)}, bf16[256,16,1,128]{3,2,1,0:T(2,128)(2,1)}, u32[]{:S(2)}) copy-start(bf16[256,16,1,128]{3,2,1,0:T(2,128)(2,1)} %copy-done.4) | copy-start | bytes 3145732
  200.6 7.2 %copy-start = (bf16[256,16,1,128]{3,2,1,0:T(2,128)(2,1)}, bf16[256,16,1,128]{3,2,1,0:T(2,128)(2,1)S(1)}, u32[]{:S(2)}) copy-start(bf16[256,16,1,128]{3,2,1,0:T(2,128)(2,1)S(1)} %get-tuple-element.10) | copy-start | bytes 3145732
  200.6 7.2 %copy-start.3 = (bf16[256,16,1,128]{3,2,1,0:T(2,128)(2,1)S(1)}, bf16[256,16,1,128]{3,2,1,0:T(2,128)(2,1)}, u32[]{:S(2)}) copy-start(bf16[256,16,1,128]{3,2,1,0:T(2,128)(2,1)} %copy-done.2) | copy-start | bytes 3145732
  286.3 8.8 %copy-start.1 = (bf16[256,16,1,128]{3,2,1,0:T(2,128)(2,1)S(1)}, bf16[256,16,1,128]{3,2,1,0:T(2,128)(2,1)}, u32[]{:S(2)}) copy-start(bf16[256,16,1,128]{3,2,1,0:T(2,128)(2,1)} %copy-done) | copy-start | bytes 3145732
  295.1 39.4 %copy-start.8 = (f32[1,16,128]{2,1,0:T(8,128)S(1)}, f32[1,16,128]{2,1,0:T(8,128)}, u32[]{:S(2)}) copy-start(f32[1,16,128]{2,1,0:T(8,128)} %param.10) | copy-start | bytes 24580
  295.1 39.4 %copy-start.9 = (f32[1,16,128]{2,1,0:T(8,128)S(1)}, f32[1,16,128]{2,1,0:T(8,128)}, u32[]{:S(2)}) copy-start(f32[1,16,128]{2,1,0:T(8,128)} %param.12) | copy-start | bytes 24580
  295.1 39.4 %copy-start.10 = (f32[1,16,128]{2,1,0:T(8,128)S(1)}, f32[1,16,128]{2,1,0:T(8,128)}, u32[]{:S(2)}) copy-start(f32[1,16,128]{2,1,0:T(8,128)} %param.11) | copy-start | bytes 24580
  334.6 13.2 %collective-permute-start.2 = (f32[16,128]{1,0:T(8,128)S(1)}, f32[16,128]{1,0:T(8,128)S(1)}, u32[]{:S(2)}, u32[]{:S(2)}) collective-permute-start(f32[16,128]{1,0:T(8,128)S(1)} %fusion.17), channel_id=1, source_target_pairs={{0,16},{16,0},{1,17},{17,1},{2,18},{18,2},{3,19},{19,3},{4,20},{20... | collective-permute-start | bytes 24584 | tf_op jit(solution)/shard_map/ppermute | solution.py:17
Sparse Core Ops, SparseCore 0:
  294.5 36.4 all-gather.2
